TPU v7x, 32 devices: a whole 2x2x4 slice. The times are simulated.
32 devices in a mesh: samp: 1, vert: 32 (over z, y, x, core).
Axes of the slice: x: 2, y: 2, z: 4, core: 2. Of those that a mesh axis runs over, the one named last changes fastest.
Arguments:
- inputs: bfloat16 [2, 131072, 128], P('samp', 'vert'), may hold values from -6 to 6
- cotangent: bfloat16 [2, 131072, 128], P('samp', 'vert'), may hold values from -6 to 6
- basis: bfloat16 [131072, 1024], P('vert'), may hold values from -0.03125 to 0.03125
- mode_weights: bfloat16 [1024, 128, 128], P('vert'), may hold values from -0.5 to 0.5
- w_up: bfloat16 [128, 512], replicated, may hold values from -0.5 to 0.5
- b_up: float32 [512], replicated, may hold values from -4 to 4
- w_down: bfloat16 [512, 128], replicated, may hold values from -0.25 to 0.25
Outputs:
- grad_input: bfloat16 [2, 131072, 128], P('samp', 'vert')
- grad_modes: float32 [1024, 128, 128], P('vert')
- grad_w_up: float32 [128, 512], replicated
- grad_b_up: float32 [512], replicated
- grad_w_down: float32 [512, 128], replicated
All inputs are finite; a program needn't handle non-finite values.
Results may differ from a plain program's by a relative error of at most 0.0055.
Values may be sent and summed in bfloat16 or wider, within the bound.
A program may use at most 128 MiB of HBM per device.

v0:
```python
import functools

import jax
import jax.numpy as jnp
from jax import lax
from jax.experimental import pallas as pl
from jax.experimental.pallas import tpu as pltpu
from jax.sharding import PartitionSpec as P

F32 = jnp.float32
BF16 = jnp.bfloat16
MESH = pl.DeviceIdType.MESH
ROOT = 0.7978845608
CUBE = 0.044715


def radices_of(size):
    radices = []
    if size % 4 == 0:
        radices.append(4)
        size //= 4
    while size > 1:
        step = 2 if size % 2 == 0 else size
        radices.append(step)
        size //= step
    return tuple(radices) or (1,)


def dot(left, right, contract):
    return lax.dot_general(left, right, (contract, ((), ())), preferred_element_type=F32)


def layer_kernel(
    plan,
    inputs_hbm, cotangent_hbm, basis_hbm, modes_hbm, w_up, b_up, w_down,
    grad_input_hbm, grad_modes_hbm, grad_up, grad_bias, grad_down,
    xs, cs, xt, basis, modes, acc, pointwise, result, outer,
    up_acc, down_acc, bias_acc, gathered, natural, left_rows, right_rows, mixed,
    weights_all, in_sems, out_sems, send_sems, recv_sems, *stages,
):
    size, radices = plan["size"], plan["radices"]
    samples, here, chan = xs.shape
    hidden_units = w_up.shape[1]
    total_modes = basis.shape[1]
    owned = total_modes // size
    depth = len(radices)
    orders = plan["orders"]
    tracks = range(len(orders))
    kinds = [stages[at * depth:(at + 1) * depth] for at in range(len(stages) // depth)]
    coef_f32, coef_send, coef_recv = kinds[0:2], kinds[2:4], kinds[4:6]
    weight_f32, weight_send, weight_recv = kinds[6:8], kinds[8:10], kinds[10:12]
    bias_slots = kinds[12]

    me = lax.axis_index("vert")
    strides = [1] * depth
    for at in range(depth - 2, -1, -1):
        strides[at] = strides[at + 1] * radices[at + 1]
    digits = [lax.rem(lax.div(me, strides[at]), radices[at]) for at in range(depth)]

    def peer(at, shift):
        digit = lax.rem(digits[at] + shift, radices[at])
        return digit, {"vert": me + (digit - digits[at]) * strides[at]}

    load_steps = plan["load_steps"]
    load_rows = here // load_steps

    def loads(step):
        rows = pl.ds(pl.multiple_of(step * load_rows, load_rows), load_rows)
        return (
            pltpu.make_async_copy(inputs_hbm.at[:, rows], xs.at[:, rows], in_sems.at[0, step]),
            pltpu.make_async_copy(cotangent_hbm.at[:, rows], cs.at[:, rows], in_sems.at[1, step]),
            pltpu.make_async_copy(basis_hbm.at[rows], basis.at[rows], in_sems.at[2, step]),
        )

    for step in range(load_steps):
        for copy in loads(step):
            copy.start()
    modes_copy = pltpu.make_async_copy(modes_hbm, modes, in_sems.at[3, 0])
    modes_copy.start()

    barrier = pltpu.get_barrier_semaphore()
    peers = 0
    for at in range(depth):
        for shift in range(1, radices[at]):
            pl.semaphore_signal(barrier, inc=1, device_id=peer(at, shift)[1], device_id_type=MESH)
            peers += 1

    acc[...] = jnp.zeros_like(acc)
    up_acc[...] = jnp.zeros_like(up_acc)
    down_acc[...] = jnp.zeros_like(down_acc)
    bias_acc[...] = jnp.zeros_like(bias_acc)

    def project(step, carry):
        for copy in loads(step):
            copy.wait()
        rows = pl.ds(pl.multiple_of(step * load_rows, load_rows), load_rows)
        for s in range(samples):
            xt[2 * s * chan:(2 * s + 1) * chan, rows] = xs[s, rows, :].T
            xt[(2 * s + 1) * chan:(2 * s + 2) * chan, rows] = cs[s, rows, :].T
        acc[...] += dot(xt[:, rows], basis[rows, :], ((1,), (0,)))
        return carry

    lax.fori_loop(0, load_steps, project, 0)

    def digits_of(owner, order):
        return [(owner // strides[at]) % radices[at] for at in order]

    def slot_of(owner, order):
        found = digits_of(owner, order)
        rest, scale = 0, 1
        for at, digit in zip(order[1:], found[1:]):
            rest += digit * scale
            scale *= radices[at]
        return found[0], rest

    half = acc.shape[0] // len(orders)
    for block in range(total_modes // 128):
        for track in tracks:
            tile = acc[track * half:(track + 1) * half, block * 128:(block + 1) * 128].T
            for part in range(128 // owned):
                owner = block * (128 // owned) + part
                coef_f32[track][0][slot_of(owner, orders[track])] = tile[part * owned:(part + 1) * owned]

    pl.semaphore_wait(barrier, peers)

    sem_at = [0]

    def exchange(at, pairs):
        copies = []
        for shift in range(1, radices[at]):
            digit, target = peer(at, shift)
            for source_of, dest in pairs:
                copies.append(pltpu.make_async_remote_copy(
                    src_ref=source_of(digit),
                    dst_ref=dest,
                    send_sem=send_sems.at[sem_at[0]],
                    recv_sem=recv_sems.at[sem_at[0]],
                    device_id=target,
                    device_id_type=MESH,
                ))
                sem_at[0] += 1
        for copy in copies:
            copy.start()
        return copies

    def finish(copies):
        for copy in copies:
            copy.wait()

    def scatter_start(turn, held, sent, got):
        copies = []
        for track in tracks:
            at = orders[track][turn]
            source = (held if turn == 0 else sent)[track][turn]
            copies += exchange(at, [(lambda digit: source.at[digit], got[track][turn].at[digits[at]])])
        return copies

    def scatter_sum(turn, copies, held, sent, got, done):
        finish(copies)
        for track in tracks:
            order = orders[track]
            at = order[turn]
            for block in range(held[track][turn].shape[1]):
                value = held[track][turn][digits[at], block]
                for shift in range(1, radices[at]):
                    value = value + got[track][turn][peer(at, shift)[0], block].astype(F32)
                if turn + 1 < depth:
                    radix = radices[order[turn + 1]]
                    held[track][turn + 1][block % radix, block // radix] = value
                    sent[track][turn + 1][block % radix, block // radix] = value.astype(BF16)
                else:
                    done(track, value)

    mine = [tuple(digits[at] for at in order) for order in orders]

    def keep_weights(track, value):
        weights_all[(track,) + mine[track]] = value.astype(BF16)

    def weights_start(turn):
        at = orders[0][turn]
        slot = bias_slots[turn].at[digits[at]]
        return scatter_start(turn, weight_f32, weight_send, weight_recv) + exchange(at, [(lambda digit: slot, slot)])

    def weights_sum(turn, copies):
        scatter_sum(turn, copies, weight_f32, weight_send, weight_recv, keep_weights)
        bias = bias_slots[turn][0]
        for slot in range(1, radices[orders[0][turn]]):
            bias = bias + bias_slots[turn][slot]
        if turn + 1 < depth:
            bias_slots[turn + 1][digits[orders[0][turn + 1]]] = bias
        else:
            grad_bias[...] = jnp.sum(bias, axis=0, keepdims=True)

    def gather_start(turn, ref):
        copies = []
        for track in tracks:
            order = orders[track]
            held = ref.at[(track,) + mine[track][:depth - turn]]
            copies += exchange(order[depth - 1 - turn], [(lambda digit: held, held)])
        return copies

    chunk = plan["chunk"]
    chunks = here // chunk

    def point(step, carry):
        rows = pl.ds(pl.multiple_of(step * chunk, chunk), chunk)
        for s in range(samples):
            z = dot(xs[s, rows, :], w_up[...], ((1,), (0,))) + b_up[...]
            square = z * z
            t = jnp.tanh(z * (ROOT + (ROOT * CUBE) * square))
            middle = 0.5 * z
            plus = 1.0 + t
            hidden = (middle * plus).astype(BF16)
            slope = plus * (0.5 + middle * (1.0 - t) * (ROOT + (3.0 * ROOT * CUBE) * square))
            grad_hidden = dot(cs[s, rows, :], w_down[...], ((1,), (1,)))
            grad_pre = (grad_hidden * slope).astype(BF16)
            pointwise[s, rows, :] = dot(grad_pre, w_up[...], ((1,), (1,)))
            up_acc[...] += dot(xt[2 * s * chan:(2 * s + 1) * chan, rows], grad_pre, ((1,), (0,)))
            down_acc[...] += dot(xt[(2 * s + 1) * chan:(2 * s + 2) * chan, rows], hidden, ((1,), (0,)))
            bias_acc[...] += jnp.sum(grad_pre.astype(F32).reshape(chunk // 8, 8, hidden_units), axis=0)
        return carry

    totals = []
    for turn in range(depth):
        copies = scatter_start(turn, coef_f32, coef_send, coef_recv)
        lax.fori_loop(chunks * turn // depth, chunks * (turn + 1) // depth, point, 0)
        scatter_sum(turn, copies, coef_f32, coef_send, coef_recv, lambda track, value: totals.append(value))
    owned_sums = jnp.concatenate(totals, axis=1)

    columns = plan["columns"]
    rows_each = 2 * chan * columns // size
    wide = hidden_units // columns
    part_wide = wide // len(orders)
    for owner in range(size):
        row = (owner // columns) * rows_each
        source = up_acc if row < chan else down_acc
        row = row % chan
        column = (owner % columns) * wide
        for track in tracks:
            start = column + track * part_wide
            weight_f32[track][0][slot_of(owner, orders[track])] = source[row:row + rows_each, start:start + part_wide]
    bias_slots[0][digits[orders[0][0]]] = bias_acc[...]

    weight_copies = weights_start(0)

    left_rows[...] = jnp.zeros_like(left_rows)
    right_rows[...] = jnp.zeros_like(right_rows)
    for s in range(samples):
        coef = owned_sums[:, 2 * s * chan:(2 * s + 1) * chan]
        grad = owned_sums[:, (2 * s + 1) * chan:(2 * s + 2) * chan]
        coef_high = coef.astype(BF16).astype(F32)
        grad_high = grad.astype(BF16).astype(F32)
        left_rows[:, s, :] = coef_high
        left_rows[:, samples + s, :] = coef_high
        left_rows[:, 2 * samples + s, :] = coef - coef_high
        right_rows[:, s, :] = grad_high
        right_rows[:, samples + s, :] = grad - grad_high
        right_rows[:, 2 * samples + s, :] = grad_high
    modes_copy.wait()
    for k in range(owned):
        mixed[k] = dot(right_rows[k].astype(BF16), modes[k], ((1,), (1,)))
    value = jnp.concatenate([mixed[:, s, :] + mixed[:, samples + s, :] for s in range(samples)], axis=1)
    part_chan = samples * chan // len(orders)
    for track in tracks:
        gathered[(track,) + mine[track]] = value[:, track * part_chan:(track + 1) * part_chan].astype(BF16)

    per_turn = -(-owned // depth)
    for turn in range(depth):
        coef_copies = gather_start(turn, gathered)
        for k in range(turn * per_turn, min(owned, (turn + 1) * per_turn)):
            outer[k] = dot(left_rows[k].astype(BF16), right_rows[k].astype(BF16), ((0,), (0,)))
        if turn + 1 == depth:
            outer_copy = pltpu.make_async_copy(outer, grad_modes_hbm, out_sems.at[1, 0])
            outer_copy.start()
        weights_sum(turn, weight_copies)
        if turn + 1 < depth:
            weight_copies = weights_start(turn + 1)
        finish(coef_copies)

    for owner in range(size):
        for track in tracks:
            natural[owner * owned:(owner + 1) * owned, track * part_chan:(track + 1) * part_chan] = gathered[
                (track,) + tuple(digits_of(owner, orders[track]))]

    def spread(step, carry):
        rows = pl.ds(pl.multiple_of(step * chunk, chunk), chunk)
        value = dot(basis[rows, :], natural[...], ((1,), (0,)))
        for s in range(samples):
            result[s, rows, :] = (value[:, s * chan:(s + 1) * chan] + pointwise[s, rows, :]).astype(BF16)
        pltpu.make_async_copy(result.at[:, rows], grad_input_hbm.at[:, rows], out_sems.at[0, step]).start()
        return carry

    for turn in range(depth):
        weight_copies = gather_start(turn, weights_all)
        lax.fori_loop(chunks * turn // depth, chunks * (turn + 1) // depth, spread, 0)
        finish(weight_copies)

    for owner in range(size):
        row = (owner // columns) * rows_each
        target = grad_up if row < chan else grad_down
        row = row % chan
        column = (owner % columns) * wide
        for track in tracks:
            start = column + track * part_wide
            target[row:row + rows_each, start:start + part_wide] = weights_all[
                (track,) + tuple(digits_of(owner, orders[track]))].astype(F32)

    for step in range(chunks):
        rows = pl.ds(step * chunk, chunk)
        pltpu.make_async_copy(result.at[:, rows], grad_input_hbm.at[:, rows], out_sems.at[0, step]).wait()
    outer_copy.wait()


def place_kernel(
    steps, input_from, modes_from, up_from, bias_from, down_from,
    input_to, modes_to, up_to, bias_to, down_to, input_held, modes_held, sems,
):
    def parts(step):
        rows = input_held.shape[1] // steps
        here = pl.ds(step * rows, rows)
        kept = modes_held.shape[0] // steps
        modes = pl.ds(step * kept, kept)
        return (
            (input_from.at[:, here], input_held.at[:, here], input_to.at[:, here]),
            (modes_from.at[modes], modes_held.at[modes], modes_to.at[modes]),
        )

    reads, writes = [], []
    for step in range(steps):
        for kind, (source, held, target) in enumerate(parts(step)):
            reads.append(pltpu.make_async_copy(source, held, sems.at[kind, step]))
            writes.append(pltpu.make_async_copy(held, target, sems.at[2 + kind, step]))
    for copy in reads:
        copy.start()
    up_to[...] = up_from[...]
    bias_to[...] = bias_from[...]
    down_to[...] = down_from[...].T
    for read, write in zip(reads, writes):
        read.wait()
        write.start()
    for write in writes:
        write.wait()


def per_device(size, inputs, cotangent, basis, mode_weights, w_up, b_up, w_down):
    samples, here, chan = inputs.shape
    hidden_units = w_up.shape[1]
    total_modes = basis.shape[1]
    owned = total_modes // size
    radices = radices_of(size)
    depth = len(radices)
    chunk = min(512, here)
    load_steps = 4
    columns = max(1, min(16 * size // (2 * chan), hidden_units // 256))
    rows_each = 2 * chan * columns // size
    wide = hidden_units // columns
    plan = {
        "size": size, "radices": radices, "chunk": chunk,
        "load_steps": load_steps, "columns": columns,
    }
    width = 2 * samples * chan
    straight = list(reversed(range(depth)))
    crossed = list(straight)
    if depth > 2:
        crossed[1], crossed[2] = crossed[2], crossed[1]
    orders = (tuple(straight), tuple(crossed))
    plan["orders"] = orders
    shapes = []
    for order in orders:
        left, found = size, []
        for at in order:
            left //= radices[at]
            found.append((radices[at], left))
        shapes.append(found)
    rows8 = 8 * (-(-3 * samples // 8))
    backwards = tuple(radices[at] for at in orders[0])
    other = tuple(radices[at] for at in orders[1])
    assert backwards == other
    copies = 9 * sum(radix - 1 for radix in radices)
    vmem = pltpu.VMEM
    scratch = [
        vmem((samples, here, chan), BF16),
        vmem((samples, here, chan), BF16),
        vmem((width, here), BF16),
        vmem((here, total_modes), BF16),
        vmem((owned, chan, chan), BF16),
        vmem((width, total_modes), F32),
        vmem((samples, here, chan), F32),
        vmem((samples, here, chan), BF16),
        vmem((owned, chan, chan), F32),
        vmem((chan, hidden_units), F32),
        vmem((chan, hidden_units), F32),
        vmem((8, hidden_units), F32),
        vmem((2,) + backwards + (owned, samples * chan // 2), BF16),
        vmem((total_modes, samples * chan), BF16),
        vmem((owned, rows8, chan), F32),
        vmem((owned, rows8, chan), F32),
        vmem((owned, rows8, chan), F32),
        vmem((2,) + backwards + (rows_each, wide // 2), BF16),
        pltpu.SemaphoreType.DMA((4, load_steps)),
        pltpu.SemaphoreType.DMA((2, here // chunk)),
        pltpu.SemaphoreType.DMA((copies,)),
        pltpu.SemaphoreType.DMA((copies,)),
    ]

    def stage_buffers(tail, first_type, later_type):
        return [
            vmem(shape + tail, later_type if turn else first_type)
            for found in shapes for turn, shape in enumerate(found)
        ]

    for tail in ((owned, width // 2), (rows_each, wide // 2)):
        scratch += stage_buffers(tail, F32, F32)
        scratch += stage_buffers(tail, BF16, BF16)
        scratch += stage_buffers(tail, F32, BF16)
    scratch += [vmem((shape[0], 8, hidden_units), F32) for shape in shapes[0]]
    anywhere = pl.BlockSpec(memory_space=pl.ANY)
    inside = pl.BlockSpec(memory_space=pltpu.VMEM)
    grad_input, grad_modes, grad_up, grad_bias, grad_down = pl.pallas_call(
        functools.partial(layer_kernel, plan),
        out_shape=(
            jax.ShapeDtypeStruct((samples, here, chan), BF16),
            jax.ShapeDtypeStruct((owned, chan, chan), F32),
            jax.ShapeDtypeStruct((chan, hidden_units), F32),
            jax.ShapeDtypeStruct((1, hidden_units), F32),
            jax.ShapeDtypeStruct((chan, hidden_units), F32),
        ),
        in_specs=[anywhere] * 4 + [inside] * 3,
        out_specs=(anywhere, anywhere, inside, inside, inside),
        scratch_shapes=scratch,
        compiler_params=pltpu.CompilerParams(
            collective_id=0, has_side_effects=True, vmem_limit_bytes=62 * 1024 * 1024
        ),
        name="layer",
    )(inputs, cotangent, basis, mode_weights, w_up, b_up.reshape(1, hidden_units), w_down)
    steps = 4
    grad_input, grad_modes, grad_up, grad_bias, grad_down = pl.pallas_call(
        functools.partial(place_kernel, steps),
        out_shape=(
            jax.ShapeDtypeStruct((samples, here, chan), BF16),
            jax.ShapeDtypeStruct((owned, chan, chan), F32),
            jax.ShapeDtypeStruct((chan, hidden_units), F32),
            jax.ShapeDtypeStruct((1, hidden_units), F32),
            jax.ShapeDtypeStruct((hidden_units, chan), F32),
        ),
        in_specs=[anywhere] * 2 + [inside] * 3,
        out_specs=(anywhere, anywhere, inside, inside, inside),
        scratch_shapes=[
            vmem((samples, here, chan), BF16),
            vmem((owned, chan, chan), F32),
            pltpu.SemaphoreType.DMA((4, steps)),
        ],
        compiler_params=pltpu.CompilerParams(vmem_limit_bytes=62 * 1024 * 1024),
        name="place",
    )(grad_input, grad_modes, grad_up, grad_bias, grad_down)
    return grad_input, grad_modes, grad_up, grad_bias.reshape(hidden_units), grad_down


def solution(mesh):
    size = mesh.shape["vert"]
    groups = mesh.shape["samp"]

    def body(*arguments):
        grad_input, grad_modes, grad_up, grad_bias, grad_down = per_device(size, *arguments)
        if groups > 1:
            grad_modes, grad_up, grad_bias, grad_down = lax.psum(
                (grad_modes, grad_up, grad_bias, grad_down), "samp"
            )
        return grad_input, grad_modes, grad_up, grad_bias, grad_down

    in_specs = (
        P("samp", "vert", None),
        P("samp", "vert", None),
        P("vert", None),
        P("vert", None, None),
        P(),
        P(),
        P(),
    )
    out_specs = (P("samp", "vert", None), P("vert", None, None), P(), P(), P())
    return jax.shard_map(body, mesh=mesh, in_specs=in_specs, out_specs=out_specs, check_vma=False)
```

profile of v0, /device:TPU:0, one launch (start us, length us, event | category | flops | bytes accessed | tf_op | source)
XLA Modules:
  0.0 62.3 jit_solution(8829487603135192992)
XLA Ops:
  0.6 56.2 %layer.1 = (bf16[2,4096,128]{2,1,0:T(8,128)(2,1)}, f32[32,128,128]{2,1,0:T(8,128)}, f32[128,512]{1,0:T(8,128)}, f32[1,512]{1,0:T(1,128)}, f32[128,512]{1,0:T(8,128)}) custom-call(bf16[2,4096,128]{2,1,0:T(8,128)(2,1)} %inputs_hbm.1, bf16[2,4096,128]{2,1,0:T(8,128)(2,1)} %cotangent_hbm.1, bf16[4096,1024]{1,0:T(8,128)(2,1)} %basis_hbm.1, ...), custom_call_target="tpu_custom_call" | custom-call | tf_op jit(solution)/shard_map/layer/pallas_call | solution.py:419
  56.9 5.4 %place.1 = (bf16[2,4096,128]{2,1,0:T(8,128)(2,1)}, f32[32,128,128]{2,1,0:T(8,128)}, f32[128,512]{1,0:T(8,128)}, f32[1,512]{1,0:T(1,128)}, f32[512,128]{1,0:T(8,128)}) custom-call(bf16[2,4096,128]{2,1,0:T(8,128)(2,1)} %get-tuple-element.15.input_from, f32[32,128,128]{2,1,0:T(8,128)} %get-tuple-element.16.modes_from, f32[128,512]{1,0:T(8,128)} %get-tuple-element.17.up_from, ...), custom_call_target="tpu_custom_call" | custom-call | tf_op jit(solution)/shard_map/place/pallas_call | solution.py:437
where the time goes:
time: 62.5 us; the launch traced here: 62.3 us
  Pallas kernels  61.7 us (99%)
  between operations  0.64 us (1%)
    pallas_call x1, Pallas kernels, per_device(): pl.pallas_call(functools.partial(layer_kernel, plan), out_shape=(jax.Shap...  56.2 us
    pallas_call x1, Pallas kernels, per_device(): pl.pallas_call(functools.partial(place_kernel, steps), out_shape=(jax.Sha...  5.4 us

commit v1 on v0

v1 whole, which is shorter than its diff:
```python
import functools

import jax
import jax.numpy as jnp
from jax import lax
from jax.experimental import pallas as pl
from jax.experimental.pallas import tpu as pltpu
from jax.sharding import PartitionSpec as P

F32 = jnp.float32
BF16 = jnp.bfloat16
MESH = pl.DeviceIdType.MESH
ROOT = 0.7978845608
CUBE = 0.044715


def reduce_radices(size):
    return (size // 8, 4, 2) if size % 16 == 0 else gather_radices(size)


def gather_radices(size):
    return (size // 2, 2) if size % 4 == 0 else (size,)


def staged(radices, size):
    left, found = size, []
    for radix in reversed(radices):
        left //= radix
        found.append((radix, left))
    return found


def dot(left, right, contract):
    return lax.dot_general(left, right, (contract, ((), ())), preferred_element_type=F32)


class Grid:
    def __init__(self, me, radices):
        self.me, self.radices, self.depth = me, radices, len(radices)
        self.strides = [1] * self.depth
        for at in range(self.depth - 2, -1, -1):
            self.strides[at] = self.strides[at + 1] * radices[at + 1]
        self.digits = [lax.rem(lax.div(me, self.strides[at]), radices[at]) for at in range(self.depth)]
        self.order = tuple(reversed(range(self.depth)))
        self.mine = tuple(self.digits[at] for at in self.order)

    def peer(self, at, shift):
        digit = lax.rem(self.digits[at] + shift, self.radices[at])
        return digit, {"vert": self.me + (digit - self.digits[at]) * self.strides[at]}

    def digits_of(self, owner):
        return tuple((owner // self.strides[at]) % self.radices[at] for at in self.order)

    def slot_of(self, owner):
        found = self.digits_of(owner)
        rest, scale = 0, 1
        for at, digit in zip(self.order[1:], found[1:]):
            rest += digit * scale
            scale *= self.radices[at]
        return found[0], rest


def layer_kernel(
    plan,
    inputs_hbm, cotangent_hbm, basis_hbm, modes_hbm, w_up_hbm, b_up_hbm, w_down_hbm,
    grad_input, grad_modes, grad_up, grad_bias, grad_down,
    xs, cs, xt, basis, modes, w_up, b_up, w_down, acc, pointwise,
    up_acc, down_acc, bias_acc, gathered, natural, left_rows, right_rows, mixed,
    weights_all, in_sems, send_sems, recv_sems, *stages,
):
    size = plan["size"]
    samples, here, chan = xs.shape
    hidden_units = w_up.shape[1]
    total_modes = basis.shape[1]
    owned = total_modes // size
    me = lax.axis_index("vert")
    reduce, gather = Grid(me, plan["reduce"]), Grid(me, plan["gather"])
    pool = list(stages)

    def take(count):
        found = pool[:count]
        del pool[:count]
        return found

    coef_held = [take(reduce.depth) for _ in range(samples)]
    coef_sent = [take(reduce.depth) for _ in range(samples)]
    coef_got = [take(reduce.depth) for _ in range(samples)]
    weight_held, weight_sent, weight_got = take(gather.depth), take(gather.depth), take(gather.depth)
    bias_slots = take(gather.depth)

    load_steps = plan["load_steps"]
    load_rows = here // load_steps

    def row_block(step):
        return pl.ds(pl.multiple_of(step * load_rows, load_rows), load_rows)

    def field_loads(s, step):
        rows = row_block(step)
        return (
            pltpu.make_async_copy(inputs_hbm.at[s, rows], xs.at[s, rows], in_sems.at[2 * s, step]),
            pltpu.make_async_copy(cotangent_hbm.at[s, rows], cs.at[s, rows], in_sems.at[2 * s + 1, step]),
        )

    def basis_load(step):
        rows = row_block(step)
        return pltpu.make_async_copy(basis_hbm.at[rows], basis.at[rows], in_sems.at[2 * samples, step])

    small_copies = [
        pltpu.make_async_copy(source, target, in_sems.at[2 * samples + 1 + at, 0])
        for at, (source, target) in enumerate(
            ((w_up_hbm, w_up), (b_up_hbm, b_up), (w_down_hbm, w_down), (modes_hbm, modes)))
    ]
    for step in range(load_steps):
        for copy in field_loads(0, step):
            copy.start()
        basis_load(step).start()
    for s in range(1, samples):
        for step in range(load_steps):
            for copy in field_loads(s, step):
                copy.start()
    for copy in small_copies:
        copy.start()

    barrier = pltpu.get_barrier_semaphore()
    peers = 0
    for at in range(gather.depth):
        for shift in range(1, gather.radices[at]):
            pl.semaphore_signal(barrier, inc=1, device_id=gather.peer(at, shift)[1], device_id_type=MESH)
            peers += 1

    acc[...] = jnp.zeros_like(acc)
    up_acc[...] = jnp.zeros_like(up_acc)
    down_acc[...] = jnp.zeros_like(down_acc)
    bias_acc[...] = jnp.zeros_like(bias_acc)
    left_rows[...] = jnp.zeros_like(left_rows)
    right_rows[...] = jnp.zeros_like(right_rows)

    sem_at = [0]

    def exchange(grid, at, pairs):
        copies = []
        for shift in range(1, grid.radices[at]):
            digit, target = grid.peer(at, shift)
            for source_of, dest in pairs:
                copies.append(pltpu.make_async_remote_copy(
                    src_ref=source_of(digit),
                    dst_ref=dest,
                    send_sem=send_sems.at[sem_at[0]],
                    recv_sem=recv_sems.at[sem_at[0]],
                    device_id=target,
                    device_id_type=MESH,
                ))
                sem_at[0] += 1
        for copy in copies:
            copy.start()
        return copies

    def finish(copies):
        for copy in copies:
            copy.wait()

    def scatter_start(grid, turn, held, sent, got):
        at = grid.order[turn]
        source = (held if turn == 0 else sent)[turn]
        return exchange(grid, at, [(lambda digit: source.at[digit], got[turn].at[grid.digits[at]])])

    def scatter_sum(grid, turn, copies, held, sent, got):
        finish(copies)
        at = grid.order[turn]
        for block in range(held[turn].shape[1]):
            value = held[turn][grid.digits[at], block]
            for shift in range(1, grid.radices[at]):
                value = value + got[turn][grid.peer(at, shift)[0], block].astype(F32)
            if turn + 1 == grid.depth:
                return value
            radix = grid.radices[grid.order[turn + 1]]
            held[turn + 1][block % radix, block // radix] = value
            sent[turn + 1][block % radix, block // radix] = value.astype(BF16)

    def gather_start(grid, turn, ref):
        held = ref.at[grid.mine[:grid.depth - turn]]
        return exchange(grid, grid.order[grid.depth - 1 - turn], [(lambda digit: held, held)])

    chunk = plan["chunk"]
    chunks = here // chunk
    done_chunks = [0]

    def point(step, carry):
        rows = pl.ds(pl.multiple_of(step * chunk, chunk), chunk)
        for s in range(samples):
            z = dot(xs[s, rows, :], w_up[...], ((1,), (0,))) + b_up[...]
            square = z * z
            t = jnp.tanh(z * (ROOT + (ROOT * CUBE) * square))
            middle = 0.5 * z
            plus = 1.0 + t
            hidden = (middle * plus).astype(BF16)
            slope = plus * (0.5 + middle * (1.0 - t) * (ROOT + (3.0 * ROOT * CUBE) * square))
            grad_hidden = dot(cs[s, rows, :], w_down[...], ((1,), (1,)))
            grad_pre = (grad_hidden * slope).astype(BF16)
            pointwise[s, rows, :] = dot(grad_pre, w_up[...], ((1,), (1,)))
            up_acc[...] += dot(xt[2 * s * chan:(2 * s + 1) * chan, rows], grad_pre, ((1,), (0,)))
            down_acc[...] += dot(xt[(2 * s + 1) * chan:(2 * s + 2) * chan, rows], hidden, ((1,), (0,)))
            bias_acc[...] += jnp.sum(grad_pre.astype(F32).reshape(chunk // 8, 8, hidden_units), axis=0)
        return carry

    def work(count):
        first = done_chunks[0]
        last = min(chunks, first + count)
        done_chunks[0] = last
        if last > first:
            lax.fori_loop(first, last, point, 0)

    coef_copies = [None] * samples

    def coef_start(s, turn):
        coef_copies[s] = scatter_start(reduce, turn, coef_held[s], coef_sent[s], coef_got[s])

    def coef_sum(s, turn):
        return scatter_sum(reduce, turn, coef_copies[s], coef_held[s], coef_sent[s], coef_got[s])

    for s in range(samples):
        def project(step, carry):
            if s == 0:
                basis_load(step).wait()
            for copy in field_loads(s, step):
                copy.wait()
            rows = row_block(step)
            low = 2 * s * chan
            xt[low:low + chan, rows] = xs[s, rows, :].T
            xt[low + chan:low + 2 * chan, rows] = cs[s, rows, :].T
            acc[low:low + 2 * chan] += dot(xt[low:low + 2 * chan, rows], basis[rows, :], ((1,), (0,)))
            return carry

        lax.fori_loop(0, load_steps, project, 0)
        if s == 0:
            pl.semaphore_wait(barrier, peers)
        for block in range(total_modes // 128):
            tile = acc[2 * s * chan:2 * (s + 1) * chan, block * 128:(block + 1) * 128].T
            for part in range(128 // owned):
                owner = block * (128 // owned) + part
                coef_held[s][0][reduce.slot_of(owner)] = tile[part * owned:(part + 1) * owned]
        coef_start(s, 0)
    for copy in small_copies:
        copy.wait()

    totals = [None] * samples
    mix = list(plan["mix"])
    for turn in range(reduce.depth):
        for s in range(samples):
            totals[s] = coef_sum(s, turn)
            if turn + 1 < reduce.depth:
                coef_start(s, turn + 1)
                work(mix.pop(0) if mix else 0)

    for s in range(samples):
        coef = totals[s][:, :chan]
        grad = totals[s][:, chan:]
        coef_high = coef.astype(BF16).astype(F32)
        grad_high = grad.astype(BF16).astype(F32)
        left_rows[:, s, :] = coef_high
        left_rows[:, samples + s, :] = coef_high
        left_rows[:, 2 * samples + s, :] = coef - coef_high
        right_rows[:, s, :] = grad_high
        right_rows[:, samples + s, :] = grad - grad_high
        right_rows[:, 2 * samples + s, :] = grad_high
    for k in range(owned):
        mixed[k] = dot(right_rows[k].astype(BF16), modes[k], ((1,), (1,)))
    value = jnp.concatenate([mixed[:, s, :] + mixed[:, samples + s, :] for s in range(samples)], axis=1)
    gathered[gather.mine] = value.astype(BF16)

    coef_gather = gather_start(gather, 0, gathered)
    work(chunks)

    columns = plan["columns"]
    rows_each = 2 * chan * columns // size
    wide = hidden_units // columns
    for owner in range(size):
        row = (owner // columns) * rows_each
        source = up_acc if row < chan else down_acc
        row = row % chan
        column = (owner % columns) * wide
        weight_held[0][gather.slot_of(owner)] = source[row:row + rows_each, column:column + wide]
    bias_slots[0][gather.mine[0]] = jnp.sum(bias_acc[...], axis=0, keepdims=True)

    def weights_start(turn):
        at = gather.order[turn]
        slot = bias_slots[turn].at[gather.digits[at]]
        return scatter_start(gather, turn, weight_held, weight_sent, weight_got) + exchange(
            gather, at, [(lambda digit: slot, slot)])

    def weights_sum(turn, copies):
        total = scatter_sum(gather, turn, copies, weight_held, weight_sent, weight_got)
        bias = bias_slots[turn][0]
        for slot in range(1, gather.radices[gather.order[turn]]):
            bias = bias + bias_slots[turn][slot]
        if turn + 1 < gather.depth:
            bias_slots[turn + 1][gather.digits[gather.order[turn + 1]]] = bias
        else:
            grad_bias[...] = bias
            weights_all[gather.mine] = total.astype(BF16)

    weight_copies = weights_start(0)
    for k in range(owned):
        grad_modes[k] = dot(left_rows[k].astype(BF16), right_rows[k].astype(BF16), ((0,), (0,)))
    for turn in range(gather.depth):
        weights_sum(turn, weight_copies)
        if turn + 1 < gather.depth:
            weight_copies = weights_start(turn + 1)
        if turn + 1 == gather.depth:
            weight_copies = gather_start(gather, 0, weights_all)
        finish(coef_gather)
        if turn + 1 < gather.depth:
            coef_gather = gather_start(gather, turn + 1, gathered)

    for owner in range(size):
        natural[owner * owned:(owner + 1) * owned] = gathered[gather.digits_of(owner)]

    def spread(step, carry):
        rows = pl.ds(pl.multiple_of(step * chunk, chunk), chunk)
        value = dot(basis[rows, :], natural[...], ((1,), (0,)))
        for s in range(samples):
            grad_input[s, rows, :] = (value[:, s * chan:(s + 1) * chan] + pointwise[s, rows, :]).astype(BF16)
        return carry

    lax.fori_loop(0, chunks, spread, 0)
    for turn in range(1, gather.depth):
        finish(weight_copies)
        weight_copies = gather_start(gather, turn, weights_all)
    finish(weight_copies)

    for owner in range(size):
        row = (owner // columns) * rows_each
        target = grad_up if row < chan else grad_down
        row = row % chan
        column = (owner % columns) * wide
        target[row:row + rows_each, column:column + wide] = weights_all[gather.digits_of(owner)].astype(F32)


def place_kernel(
    input_from, modes_from, up_from, bias_from, down_from,
    input_to, modes_to, up_to, bias_to, down_to, sems,
):
    copies = (
        pltpu.make_async_copy(input_from, input_to, sems.at[0]),
        pltpu.make_async_copy(modes_from, modes_to, sems.at[1]),
    )
    for copy in copies:
        copy.start()
    up_to[...] = up_from[...]
    bias_to[...] = bias_from[...]
    down_to[...] = down_from[...].T
    for copy in copies:
        copy.wait()


def per_device(size, inputs, cotangent, basis, mode_weights, w_up, b_up, w_down):
    samples, here, chan = inputs.shape
    hidden_units = w_up.shape[1]
    total_modes = basis.shape[1]
    owned = total_modes // size
    reduce, gather = reduce_radices(size), gather_radices(size)
    chunk = min(512, here)
    load_steps = 4
    columns = max(1, min(16 * size // (2 * chan), hidden_units // 256))
    rows_each = 2 * chan * columns // size
    wide = hidden_units // columns
    plan = {
        "size": size, "reduce": reduce, "gather": gather, "chunk": chunk,
        "load_steps": load_steps, "columns": columns, "mix": (1, 2, 2, 1),
    }
    width = 2 * samples * chan
    rows8 = 8 * (-(-3 * samples // 8))
    backwards = tuple(reversed(gather))
    copies = samples * sum(radix - 1 for radix in reduce) + 4 * sum(radix - 1 for radix in gather)
    vmem = pltpu.VMEM
    scratch = [
        vmem((samples, here, chan), BF16),
        vmem((samples, here, chan), BF16),
        vmem((width, here), BF16),
        vmem((here, total_modes), BF16),
        vmem((owned, chan, chan), BF16),
        vmem(w_up.shape, BF16),
        vmem((1, hidden_units), F32),
        vmem(w_down.shape, BF16),
        vmem((width, total_modes), F32),
        vmem((samples, here, chan), F32),
        vmem((chan, hidden_units), F32),
        vmem((chan, hidden_units), F32),
        vmem((8, hidden_units), F32),
        vmem(backwards + (owned, samples * chan), BF16),
        vmem((total_modes, samples * chan), BF16),
        vmem((owned, rows8, chan), F32),
        vmem((owned, rows8, chan), F32),
        vmem((owned, rows8, chan), F32),
        vmem(backwards + (rows_each, wide), BF16),
        pltpu.SemaphoreType.DMA((2 * samples + 5, load_steps)),
        pltpu.SemaphoreType.DMA((copies,)),
        pltpu.SemaphoreType.DMA((copies,)),
    ]

    def stage_buffers(radices, tail, first_type, later_type):
        return [
            vmem(shape + tail, later_type if turn else first_type)
            for turn, shape in enumerate(staged(radices, size))
        ]

    coef_tail, weight_tail = (owned, 2 * chan), (rows_each, wide)
    for first, later in ((F32, F32), (BF16, BF16), (F32, BF16)):
        for _ in range(samples):
            scratch += stage_buffers(reduce, coef_tail, first, later)
    for first, later in ((F32, F32), (BF16, BF16), (F32, BF16)):
        scratch += stage_buffers(gather, weight_tail, first, later)
    scratch += [vmem((shape[0], 1, hidden_units), F32) for shape in staged(gather, size)]
    outside = pl.BlockSpec(memory_space=pltpu.HBM)
    inside = pl.BlockSpec(memory_space=pltpu.VMEM)
    results = pl.pallas_call(
        functools.partial(layer_kernel, plan),
        out_shape=(
            jax.ShapeDtypeStruct((samples, here, chan), BF16),
            jax.ShapeDtypeStruct((owned, chan, chan), F32),
            jax.ShapeDtypeStruct((chan, hidden_units), F32),
            jax.ShapeDtypeStruct((1, hidden_units), F32),
            jax.ShapeDtypeStruct((chan, hidden_units), F32),
        ),
        in_specs=[outside] * 7,
        out_specs=(inside,) * 5,
        scratch_shapes=scratch,
        compiler_params=pltpu.CompilerParams(
            collective_id=0, has_side_effects=True, vmem_limit_bytes=44 * 1024 * 1024
        ),
        name="layer",
    )(*(pltpu.with_memory_space_constraint(x, pltpu.HBM) for x in (
        inputs, cotangent, basis, mode_weights, w_up, b_up.reshape(1, hidden_units), w_down)))
    grad_input, grad_modes, grad_up, grad_bias, grad_down = pl.pallas_call(
        place_kernel,
        out_shape=(
            jax.ShapeDtypeStruct((samples, here, chan), BF16),
            jax.ShapeDtypeStruct((owned, chan, chan), F32),
            jax.ShapeDtypeStruct((chan, hidden_units), F32),
            jax.ShapeDtypeStruct((1, hidden_units), F32),
            jax.ShapeDtypeStruct((hidden_units, chan), F32),
        ),
        in_specs=[inside] * 5,
        out_specs=(outside, outside, inside, inside, inside),
        scratch_shapes=[pltpu.SemaphoreType.DMA((2,))],
        compiler_params=pltpu.CompilerParams(vmem_limit_bytes=8 * 1024 * 1024),
        name="place",
    )(*results)
    return grad_input, grad_modes, grad_up, grad_bias.reshape(hidden_units), grad_down


def solution(mesh):
    size = mesh.shape["vert"]
    groups = mesh.shape["samp"]

    def body(*arguments):
        grad_input, grad_modes, grad_up, grad_bias, grad_down = per_device(size, *arguments)
        if groups > 1:
            grad_modes, grad_up, grad_bias, grad_down = lax.psum(
                (grad_modes, grad_up, grad_bias, grad_down), "samp"
            )
        return grad_input, grad_modes, grad_up, grad_bias, grad_down

    in_specs = (
        P("samp", "vert", None),
        P("samp", "vert", None),
        P("vert", None),
        P("vert", None, None),
        P(),
        P(),
        P(),
    )
    out_specs = (P("samp", "vert", None), P("vert", None, None), P(), P(), P())
    return jax.shard_map(body, mesh=mesh, in_specs=in_specs, out_specs=out_specs, check_vma=False)
```

time: 62.5 us -> 50.8 us (0.81)
  Pallas kernels: 61.7 us -> 49.8 us
    pallas_call x1, Pallas kernels: 56.2 us -> 47 us  [per_device(): pl.pallas_call(functools.partial(layer_kernel, plan), out_shape=(jax.Shap...]
    pallas_call x1, Pallas kernels: 5.4 us -> 2.83 us  [per_device(): pl.pallas_call(place_kernel, out_shape=(jax.ShapeDtypeStruct((samples, he...]
where the time goes in v1:
time: 50.8 us; the launch traced here: 50.6 us
  Pallas kernels  49.8 us (98%)
  between operations  0.8 us (2%)
    pallas_call x1, Pallas kernels, per_device(): pl.pallas_call(functools.partial(layer_kernel, plan), out_shape=(jax.Shap...  47 us
    pallas_call x1, Pallas kernels, per_device(): pl.pallas_call(place_kernel, out_shape=(jax.ShapeDtypeStruct((samples, he...  2.83 us

profile of v1, /device:TPU:0, one launch (start us, length us, event | category | flops | bytes accessed | tf_op | source)
XLA Modules:
  0.0 50.6 jit_solution(3261038861284264703)
XLA Ops:
  0.6 47.0 %layer.1 = (bf16[2,4096,128]{2,1,0:T(8,128)(2,1)S(1)}, f32[32,128,128]{2,1,0:T(8,128)S(1)}, f32[128,512]{1,0:T(8,128)S(1)}, f32[1,512]{1,0:T(1,128)S(1)}, f32[128,512]{1,0:T(8,128)S(1)}) custom-call(bf16[2,4096,128]{2,1,0:T(8,128)(2,1)} %inputs_hbm.1, bf16[2,4096,128]{2,1,0:T(8,128)(2,1)} %cotangent_hbm.1, bf16[4096,1024]{1,0:T(8,128)(2,1)} %basis_hbm.1, ...), custom_call_target="tpu_custom_call" | custom-call | tf_op jit(solution)/shard_map/layer/pallas_call | solution.py:416
  47.6 2.8 %place.1 = (bf16[2,4096,128]{2,1,0:T(8,128)(2,1)}, f32[32,128,128]{2,1,0:T(8,128)}, f32[128,512]{1,0:T(8,128)}, f32[1,512]{1,0:T(1,128)}, f32[512,128]{1,0:T(8,128)}) custom-call(bf16[2,4096,128]{2,1,0:T(8,128)(2,1)S(1)} %get-tuple-element.15.input_from, f32[32,128,128]{2,1,0:T(8,128)S(1)} %get-tuple-element.16.modes_from, ...), custom_call_target="tpu_custom_call" | custom-call | tf_op jit(solution)/shard_map/place/pallas_call | solution.py:434

commit v2 on v1

--- a/solution.py
+++ b/solution.py
@@ -64,7 +64,7 @@
     plan,
     inputs_hbm, cotangent_hbm, basis_hbm, modes_hbm, w_up_hbm, b_up_hbm, w_down_hbm,
     grad_input, grad_modes, grad_up, grad_bias, grad_down,
-    xs, cs, xt, basis, modes, w_up, b_up, w_down, acc, pointwise,
+    xs, cs, xt, basis, modes, w_up, b_up, w_down, w_half, b_half, acc, pointwise,
     up_acc, down_acc, bias_acc, gathered, natural, left_rows, right_rows, mixed,
     weights_all, in_sems, send_sems, recv_sems, *stages,
 ):
@@ -187,20 +187,20 @@
 
     def point(step, carry):
         rows = pl.ds(pl.multiple_of(step * chunk, chunk), chunk)
+        ones = jnp.ones((8, chunk), BF16)
         for s in range(samples):
-            z = dot(xs[s, rows, :], w_up[...], ((1,), (0,))) + b_up[...]
-            square = z * z
-            t = jnp.tanh(z * (ROOT + (ROOT * CUBE) * square))
-            middle = 0.5 * z
+            middle = dot(xs[s, rows, :], w_half[...], ((1,), (0,))) + b_half[...]
+            square = middle * middle
+            t = jnp.tanh(middle * (2.0 * ROOT + (8.0 * ROOT * CUBE) * square))
             plus = 1.0 + t
             hidden = (middle * plus).astype(BF16)
-            slope = plus * (0.5 + middle * (1.0 - t) * (ROOT + (3.0 * ROOT * CUBE) * square))
+            slope = plus * (0.5 + middle * (1.0 - t) * (ROOT + (12.0 * ROOT * CUBE) * square))
             grad_hidden = dot(cs[s, rows, :], w_down[...], ((1,), (1,)))
             grad_pre = (grad_hidden * slope).astype(BF16)
             pointwise[s, rows, :] = dot(grad_pre, w_up[...], ((1,), (1,)))
             up_acc[...] += dot(xt[2 * s * chan:(2 * s + 1) * chan, rows], grad_pre, ((1,), (0,)))
             down_acc[...] += dot(xt[(2 * s + 1) * chan:(2 * s + 2) * chan, rows], hidden, ((1,), (0,)))
-            bias_acc[...] += jnp.sum(grad_pre.astype(F32).reshape(chunk // 8, 8, hidden_units), axis=0)
+            bias_acc[...] += dot(ones, grad_pre, ((1,), (0,)))
         return carry
 
     def work(count):
@@ -242,6 +242,8 @@
         coef_start(s, 0)
     for copy in small_copies:
         copy.wait()
+    w_half[...] = w_up[...] * jnp.bfloat16(0.5)
+    b_half[...] = b_up[...] * 0.5
 
     totals = [None] * samples
     mix = list(plan["mix"])
@@ -280,7 +282,7 @@
         row = row % chan
         column = (owner % columns) * wide
         weight_held[0][gather.slot_of(owner)] = source[row:row + rows_each, column:column + wide]
-    bias_slots[0][gather.mine[0]] = jnp.sum(bias_acc[...], axis=0, keepdims=True)
+    bias_slots[0][gather.mine[0]] = bias_acc[0:1]
 
     def weights_start(turn):
         at = gather.order[turn]
@@ -338,17 +340,21 @@
 
 def place_kernel(
     input_from, modes_from, up_from, bias_from, down_from,
-    input_to, modes_to, up_to, bias_to, down_to, sems,
+    input_to, modes_to, up_to, bias_to, down_to, turned, sems,
 ):
-    copies = (
-        pltpu.make_async_copy(input_from, input_to, sems.at[0]),
-        pltpu.make_async_copy(modes_from, modes_to, sems.at[1]),
-    )
-    for copy in copies:
+    pairs = []
+    for source, target, parts in ((input_from, input_to, 2), (modes_from, modes_to, 2)):
+        rows = source.shape[-2 if source is input_from else 0] // parts
+        for part in range(parts):
+            here = pl.ds(part * rows, rows)
+            where = (slice(None), here) if source is input_from else (here,)
+            pairs.append((source.at[where], target.at[where]))
+    pairs += [(up_from, up_to), (bias_from, bias_to), (turned, down_to)]
+    copies = [pltpu.make_async_copy(*pair, sems.at[at]) for at, pair in enumerate(pairs)]
+    for copy in copies[:-1]:
         copy.start()
-    up_to[...] = up_from[...]
-    bias_to[...] = bias_from[...]
-    down_to[...] = down_from[...].T
+    turned[...] = down_from[...].T
+    copies[-1].start()
     for copy in copies:
         copy.wait()
 
@@ -366,7 +372,7 @@
     wide = hidden_units // columns
     plan = {
         "size": size, "reduce": reduce, "gather": gather, "chunk": chunk,
-        "load_steps": load_steps, "columns": columns, "mix": (1, 2, 2, 1),
+        "load_steps": load_steps, "columns": columns, "mix": (1, 2, 1, 1),
     }
     width = 2 * samples * chan
     rows8 = 8 * (-(-3 * samples // 8))
@@ -382,6 +388,8 @@
         vmem(w_up.shape, BF16),
         vmem((1, hidden_units), F32),
         vmem(w_down.shape, BF16),
+        vmem(w_up.shape, BF16),
+        vmem((1, hidden_units), F32),
         vmem((width, total_modes), F32),
         vmem((samples, here, chan), F32),
         vmem((chan, hidden_units), F32),
@@ -426,7 +434,7 @@
         out_specs=(inside,) * 5,
         scratch_shapes=scratch,
         compiler_params=pltpu.CompilerParams(
-            collective_id=0, has_side_effects=True, vmem_limit_bytes=44 * 1024 * 1024
+            collective_id=0, has_side_effects=True, vmem_limit_bytes=45 * 1024 * 1024
         ),
         name="layer",
     )(*(pltpu.with_memory_space_constraint(x, pltpu.HBM) for x in (
@@ -441,8 +449,8 @@
             jax.ShapeDtypeStruct((hidden_units, chan), F32),
         ),
         in_specs=[inside] * 5,
-        out_specs=(outside, outside, inside, inside, inside),
-        scratch_shapes=[pltpu.SemaphoreType.DMA((2,))],
+        out_specs=(outside,) * 5,
+        scratch_shapes=[vmem((hidden_units, chan), F32), pltpu.SemaphoreType.DMA((2 * 2 + 3,))],
         compiler_params=pltpu.CompilerParams(vmem_limit_bytes=8 * 1024 * 1024),
         name="place",
     )(*results)

time: 50.8 us -> 48.6 us (0.957)
  Pallas kernels: 49.8 us -> 47.8 us
    pallas_call x1, Pallas kernels: 47 us -> 45.6 us  [per_device(): pl.pallas_call(functools.partial(layer_kernel, plan), out_shape=(jax.Shap...]
    pallas_call x1, Pallas kernels: 2.83 us -> 2.24 us  [per_device(): pl.pallas_call(place_kernel, out_shape=(jax.ShapeDtypeStruct((samples, he...]
where the time goes in v2:
time: 48.6 us; the launch traced here: 48.5 us
  Pallas kernels  47.8 us (98%)
  between operations  0.64 us (1%)
    pallas_call x1, Pallas kernels, per_device(): pl.pallas_call(functools.partial(layer_kernel, plan), out_shape=(jax.Shap...  45.6 us
    pallas_call x1, Pallas kernels, per_device(): pl.pallas_call(place_kernel, out_shape=(jax.ShapeDtypeStruct((samples, he...  2.24 us

profile of v2, /device:TPU:0, one launch (start us, length us, event | category | flops | bytes accessed | tf_op | source)
XLA Modules:
  0.0 48.5 jit_solution(5359887805837449599)
XLA Ops:
  0.6 45.6 %layer.1 = (bf16[2,4096,128]{2,1,0:T(8,128)(2,1)S(1)}, f32[32,128,128]{2,1,0:T(8,128)S(1)}, f32[128,512]{1,0:T(8,128)S(1)}, f32[1,512]{1,0:T(1,128)S(1)}, f32[128,512]{1,0:T(8,128)S(1)}) custom-call(bf16[2,4096,128]{2,1,0:T(8,128)(2,1)} %inputs_hbm.1, bf16[2,4096,128]{2,1,0:T(8,128)(2,1)} %cotangent_hbm.1, bf16[4096,1024]{1,0:T(8,128)(2,1)} %basis_hbm.1, ...), custom_call_target="tpu_custom_call" | custom-call | tf_op jit(solution)/shard_map/layer/pallas_call | solution.py:424
  46.2 2.2 %place.1 = (bf16[2,4096,128]{2,1,0:T(8,128)(2,1)}, f32[32,128,128]{2,1,0:T(8,128)}, f32[128,512]{1,0:T(8,128)}, f32[1,512]{1,0:T(1,128)}, f32[512,128]{1,0:T(8,128)}) custom-call(bf16[2,4096,128]{2,1,0:T(8,128)(2,1)S(1)} %get-tuple-element.15.input_from, f32[32,128,128]{2,1,0:T(8,128)S(1)} %get-tuple-element.16.modes_from, ...), custom_call_target="tpu_custom_call" | custom-call | tf_op jit(solution)/shard_map/place/pallas_call | solution.py:442

commit v3 on v2

--- a/solution.py
+++ b/solution.py
@@ -302,12 +302,13 @@
             weights_all[gather.mine] = total.astype(BF16)
 
     weight_copies = weights_start(0)
-    for k in range(owned):
-        grad_modes[k] = dot(left_rows[k].astype(BF16), right_rows[k].astype(BF16), ((0,), (0,)))
     for turn in range(gather.depth):
         weights_sum(turn, weight_copies)
         if turn + 1 < gather.depth:
             weight_copies = weights_start(turn + 1)
+        if turn == 0:
+            for k in range(owned):
+                grad_modes[k] = dot(left_rows[k].astype(BF16), right_rows[k].astype(BF16), ((0,), (0,)))
         if turn + 1 == gather.depth:
             weight_copies = gather_start(gather, 0, weights_all)
         finish(coef_gather)

time: 48.6 us -> 48.6 us (level)
  no operation moved by 1% of the time
where the time goes in v3:
time: 48.6 us; the launch traced here: 48.5 us
  Pallas kernels  47.8 us (98%)
  between operations  0.64 us (1%)
    pallas_call x1, Pallas kernels, per_device(): pl.pallas_call(functools.partial(layer_kernel, plan), out_shape=(jax.Shap...  45.6 us
    pallas_call x1, Pallas kernels, per_device(): pl.pallas_call(place_kernel, out_shape=(jax.ShapeDtypeStruct((samples, he...  2.24 us

profile of v3, /device:TPU:0, one launch (start us, length us, event | category | flops | bytes accessed | tf_op | source)
XLA Modules:
  0.0 48.5 jit_solution(12907059990127939349)
XLA Ops:
  0.6 45.6 %layer.1 = (bf16[2,4096,128]{2,1,0:T(8,128)(2,1)S(1)}, f32[32,128,128]{2,1,0:T(8,128)S(1)}, f32[128,512]{1,0:T(8,128)S(1)}, f32[1,512]{1,0:T(1,128)S(1)}, f32[128,512]{1,0:T(8,128)S(1)}) custom-call(bf16[2,4096,128]{2,1,0:T(8,128)(2,1)} %inputs_hbm.1, bf16[2,4096,128]{2,1,0:T(8,128)(2,1)} %cotangent_hbm.1, bf16[4096,1024]{1,0:T(8,128)(2,1)} %basis_hbm.1, ...), custom_call_target="tpu_custom_call" | custom-call | tf_op jit(solution)/shard_map/layer/pallas_call | solution.py:425
  46.2 2.2 %place.1 = (bf16[2,4096,128]{2,1,0:T(8,128)(2,1)}, f32[32,128,128]{2,1,0:T(8,128)}, f32[128,512]{1,0:T(8,128)}, f32[1,512]{1,0:T(1,128)}, f32[512,128]{1,0:T(8,128)}) custom-call(bf16[2,4096,128]{2,1,0:T(8,128)(2,1)S(1)} %get-tuple-element.15.input_from, f32[32,128,128]{2,1,0:T(8,128)S(1)} %get-tuple-element.16.modes_from, ...), custom_call_target="tpu_custom_call" | custom-call | tf_op jit(solution)/shard_map/place/pallas_call | solution.py:443
